TPU v7x, 32 devices: a whole 2x2x4 slice. The times are simulated.
32 devices in a mesh: slab: 8 (over z, core), split: 4 (over y, x).
Axes of the slice: x: 2, y: 2, z: 4, core: 2. Of those that a mesh axis runs over, the one named last changes fastest.
Arguments:
- displacement: float32 [3, 64, 128, 256], P(None, 'slab', 'split'), may hold values from -0.3 to 0.3
- velocity: float32 [3, 64, 128, 256], P(None, 'slab', 'split'), may hold values from -0.6 to 0.6
- acceleration: float32 [3, 64, 128, 256], P(None, 'slab', 'split'), may hold values from -1.8 to 1.8
- bond_masks: int32 [4, 64, 128, 256], P(None, 'slab', 'split'), may hold values from 0 to 255, as said below
- proj_pos: float32 [32, 3, 128], replicated, may hold values from -0.5 to 257, as said below
- proj_vel: float32 [32, 3, 128], replicated, may hold values from -1.8 to 1.8
- proj_acc: float32 [32, 3, 128], replicated, may hold values from -1.8 to 1.8
- contact_pairs: int32 [3, 2, 512], P(None, None, ('slab', 'split')), may hold values from -1 to 31, as said below
Outputs:
- final_displacement: float32 [3, 64, 128, 256], P(None, 'slab', 'split')
- final_velocity: float32 [3, 64, 128, 256], P(None, 'slab', 'split')
- final_proj_pos: float32 [32, 3, 128], replicated
- final_proj_vel: float32 [32, 3, 128], replicated
Inputs may be any that keep to these rules, and one draw needn't show every extreme that they name: `bond_masks`: bit b of word w (the value divided by 2 to the b, modulo 2) is 1 where the bond from the cell to the offset numbered 8 w + b is intact. `contact_pairs`: slots d * 16 to (d + 1) * 16 - 1 belong to device d. Row 0 names one of that device's 8 surface blocks; row 1 names a projectile block, or -1 for an empty slot. Live slots come first on every device and no pair repeats on a device within a substep. In every substep each projectile block is paired on exactly one device, one of the four devices of the 2 x 2 group of device blocks under it, and on another device than in the substep before; in every substep some device has all 16 slots live. `proj_pos`: the device blocks fall into 2 x 2 groups (slab indices 2a and 2a + 1, split indices 2b and 2b + 1). Every projectile block lies above one such group, between 0.5 and 2 cells over the top layer, and every group lies under exactly 4 projectile blocks.
All inputs are finite; a program needn't handle non-finite values.
Results may differ from a plain program's by a relative error of at most 0.0003.
Values sent between devices are 32-bit elements; how exact they have to be, the bound alone decides.
A program may use at most 128 MiB of HBM per device.

v0:
```python
import math
import jax
import jax.numpy as jnp
from jax import lax
from jax.sharding import PartitionSpec as P

SUB = 3
SL = 4
PTS = 128
SB_DEV = 8
time_step = 0.25
bond_stiffness = 0.5
contact_stiffness = 0.05
contact_width = 8.0
inverse_mass = 0.5


def with_halo(cells, sides, width):
    for axis, dim in sides:
        count = lax.axis_size(axis)
        ends = count - 1
        head = lax.slice_in_dim(cells, 0, width, axis=dim)
        tail = lax.slice_in_dim(cells, cells.shape[dim] - width, cells.shape[dim], axis=dim)
        cells = jnp.concatenate(
            [
                lax.ppermute(tail, axis, [(i, (i + 1) % count) for i in range(ends)]),
                cells,
                lax.ppermute(head, axis, [((i + 1) % count, i) for i in range(ends)]),
            ],
            axis=dim,
        )
    return cells


def bond_offsets():
    listed = []
    for shift_x in (-2, -1, 0, 1, 2):
        for shift_y in (-2, -1, 0, 1, 2):
            for shift_z in (-2, -1, 0, 1, 2):
                squared = shift_x * shift_x + shift_y * shift_y + shift_z * shift_z
                if 0 < squared <= 4:
                    listed.append((shift_x, shift_y, shift_z))
    return listed


def bond_term(neighbour, displace, intact, valid_bond, offset):
    shift_x, shift_y, shift_z = offset
    length = math.sqrt(shift_x * shift_x + shift_y * shift_y + shift_z * shift_z)
    along_x = shift_x + (neighbour[0] - displace[0])
    along_y = shift_y + (neighbour[1] - displace[1])
    along_z = shift_z + (neighbour[2] - displace[2])
    squared = along_x * along_x + along_y * along_y + along_z * along_z
    stretch = (squared - length * length) / (length * (jnp.sqrt(squared) + length))
    return bond_stiffness / length * stretch * intact * valid_bond


def add_bond(bond_total, coefficient, offset):
    direction = jnp.array(offset, bond_total.dtype)
    return bond_total + direction[:, None, None, None] * coefficient[None]


def shift_depth(values_in, shift_size):
    if shift_size == 0:
        return values_in
    filler = jnp.zeros(values_in.shape[:-1] + (abs(shift_size),), values_in.dtype)
    if shift_size > 0:
        return jnp.concatenate([values_in[..., shift_size:], filler], axis=-1)
    return jnp.concatenate([filler, values_in[..., :shift_size]], axis=-1)


def bond_forces(padded, displace, mask_words, inside_x, inside_y):
    cells_x, cells_y, cells_z = (displace.shape[1], displace.shape[2], displace.shape[3])
    depth_index = jnp.arange(cells_z)
    bond_total = jnp.zeros_like(displace)
    for number, offset in enumerate(bond_offsets()):
        shift_x, shift_y, shift_z = offset
        window = padded[
            :, 2 + shift_x : 2 + shift_x + cells_x, 2 + shift_y : 2 + shift_y + cells_y, :
        ]
        neighbour = shift_depth(window, shift_z)
        moved_depth = depth_index + shift_z
        inside_z = ((moved_depth >= 0) & (moved_depth < cells_z)).astype(jnp.float32)
        valid_bond = (
            inside_x[2 + shift_x : 2 + shift_x + cells_x][:, None, None]
            * inside_y[2 + shift_y : 2 + shift_y + cells_y][None, :, None]
            * inside_z[None, None, :]
        )
        intact = (mask_words[number // 8] // 2 ** (number % 8) % 2).astype(jnp.float32)
        bond_total = add_bond(
            bond_total, bond_term(neighbour, displace, intact, valid_bond, offset), offset
        )
    return bond_total


def contact_tile(points, particles):
    separation = points[:, :, None] - particles[:, None, :]
    squared = jnp.sum(separation * separation, axis=0)
    weight = contact_stiffness * jnp.exp(-squared / contact_width)
    pulled = weight[None] * separation
    return (jnp.sum(pulled, axis=2), -jnp.sum(pulled, axis=1))


def slot_tiles(slot_points, chosen, positions):
    picked = positions[jnp.maximum(chosen, 0)]
    on_points, on_particles = jax.vmap(contact_tile)(slot_points, picked)
    live = (chosen >= 0).astype(jnp.float32)[:, None, None]
    return (on_points * live, on_particles * live)


def per_device(
    displacement, velocity, acceleration, bond_masks, proj_pos, proj_vel, proj_acc, contact_pairs
):
    cells_x, cells_y, cells_z = (
        displacement.shape[1],
        displacement.shape[2],
        displacement.shape[3],
    )
    slab_count = lax.axis_size("slab")
    split_count = lax.axis_size("split")
    corner_x = lax.axis_index("slab") * cells_x
    corner_y = lax.axis_index("split") * cells_y
    span_x = jnp.arange(-2, cells_x + 2) + corner_x
    span_y = jnp.arange(-2, cells_y + 2) + corner_y
    inside_x = ((span_x >= 0) & (span_x < slab_count * cells_x)).astype(jnp.float32)
    inside_y = ((span_y >= 0) & (span_y < split_count * cells_y)).astype(jnp.float32)
    place_x = (corner_x + jnp.arange(cells_x)).astype(jnp.float32)
    place_y = (corner_y + jnp.arange(cells_y)).astype(jnp.float32)
    place_z = (cells_z - SL + jnp.arange(SL)).astype(jnp.float32)
    lattice = jnp.stack(
        [
            jnp.broadcast_to(place_x[:, None, None], (cells_x, cells_y, SL)),
            jnp.broadcast_to(place_y[None, :, None], (cells_x, cells_y, SL)),
            jnp.broadcast_to(place_z[None, None, :], (cells_x, cells_y, SL)),
        ]
    )
    blocks_total = proj_pos.shape[0]
    particle_slots = jnp.arange(blocks_total)
    block_slots = jnp.arange(SB_DEV)
    for substep in range(SUB):
        half_velocity = velocity + 0.5 * time_step * acceleration
        displacement = displacement + time_step * half_velocity
        proj_half = proj_vel + 0.5 * time_step * proj_acc
        proj_pos = proj_pos + time_step * proj_half
        padded = with_halo(displacement, (("slab", 1), ("split", 2)), 2)
        forces = bond_forces(padded, displacement, bond_masks, inside_x, inside_y)
        top_layers = displacement[:, :, :, cells_z - SL :]
        places = (top_layers + lattice).reshape(3, SB_DEV, PTS)
        slot_pairs = contact_pairs[substep]
        targets = slot_pairs[0]
        chosen = slot_pairs[1]
        slot_points = jnp.moveaxis(jnp.take(places, targets, axis=1), 1, 0)
        on_points, on_particles = slot_tiles(slot_points, chosen, proj_pos)
        target_hits = (targets[:, None] == block_slots[None, :]).astype(jnp.float32)
        surface = jnp.einsum("ks,kcp->csp", target_hits, on_points, precision=lax.Precision.HIGHEST)
        forces = forces + jnp.pad(
            surface.reshape(3, cells_x, cells_y, SL), ((0, 0), (0, 0), (0, 0), (cells_z - SL, 0))
        )
        particle_hits = (chosen[:, None] == particle_slots[None, :]).astype(jnp.float32)
        particle_local = jnp.einsum(
            "kb,kcp->bcp", particle_hits, on_particles, precision=lax.Precision.HIGHEST
        )
        acceleration = forces
        velocity = half_velocity + 0.5 * time_step * acceleration
        particle_force = lax.psum(particle_local, ("slab", "split"))
        proj_acc = inverse_mass * particle_force
        proj_vel = proj_half + 0.5 * time_step * proj_acc
    return (displacement, velocity, proj_pos, proj_vel)


def solution(mesh):
    placed = (
        P(None, "slab", "split", None),
        P(None, "slab", "split", None),
        P(None, "slab", "split", None),
        P(None, "slab", "split", None),
        P(),
        P(),
        P(),
        P(None, None, ("slab", "split")),
    )
    return jax.shard_map(
        per_device,
        mesh=mesh,
        in_specs=placed,
        out_specs=(P(None, "slab", "split", None), P(None, "slab", "split", None), P(), P()),
        check_vma=False,
    )
```

profile of v0, /device:TPU:4, one launch (start us, length us, event | category | flops | bytes accessed | tf_op | source)
XLA Modules:
  0.0 280.0 jit_solution(2510947669306366044)
XLA Ops:
  0.6 1.8 multiply_add_fusion.3
  3.2 1.3 collective-permute-start.1
  4.5 3.0 %collective-permute-start = (f32[3,2,32,256]{3,2,1,0:T(8,128)S(1)}, f32[3,2,32,256]{3,2,1,0:T(8,128)S(1)}, u32[]{:S(2)}, u32[]{:S(2)}) collective-permute-start(f32[3,2,32,256]{3,2,1,0:T(8,128)S(1)} %get-tuple-element.217), channel_id=1, source_target_pairs={{0,4},{4,8},{8,12},{12,16},{16,20},{20,24},{24,28},{1,5},{5,9},{9,... | collective-permute-start | bytes 589832 | tf_op jit(solution)/shard_map/ppermute | solution.py:26
  10.4 1.4 fusion.1172
  14.5 1.0 fusion.6
  15.8 2.0 fusion
  18.2 1.4 copy.483
  20.0 41.7 %psum.21 = f32[32,3,128]{2,0,1:T(8,128)S(1)} all-reduce(f32[32,3,128]{2,0,1:T(8,128)S(1)} %fusion.1136), channel_id=1, replica_groups=mesh['slab'=8,'split'=4] {'slab','split'}, use_global_device_ids=true, to_apply=%region_3.5 | all-reduce | flops 12288 | bytes 98304 | tf_op jit(solution)/shard_map/psum | solution.py:164
  64.2 1.2 gather_fusion.1
  65.7 3.3 %collective-permute-start.3 = (f32[3,12,2,256]{3,2,1,0:T(2,128)S(1)}, f32[3,12,2,256]{3,2,1,0:T(2,128)S(1)}, u32[]{:S(2)}, u32[]{:S(2)}) collective-permute-start(f32[3,12,2,256]{3,2,1,0:T(2,128)S(1)} %get-tuple-element.190), channel_id=1, source_target_pairs={{1,0},{2,1},{3,2},{5,4},{6,5},{7,6},{9,8},{10,9},{11,10},{13,12},{... | collective-permute-start | bytes 221192 | tf_op jit(solution)/shard_map/ppermute | solution.py:28
  69.0 3.0 %collective-permute-start.2 = (f32[3,12,2,256]{3,2,1,0:T(2,128)S(1)}, f32[3,12,2,256]{3,2,1,0:T(2,128)S(1)}, u32[]{:S(2)}, u32[]{:S(2)}) collective-permute-start(f32[3,12,2,256]{3,2,1,0:T(2,128)S(1)} %get-tuple-element.191), channel_id=1, source_target_pairs={{0,1},{1,2},{2,3},{4,5},{5,6},{6,7},{8,9},{9,10},{10,11},{12,13},{... | collective-permute-start | bytes 221192 | tf_op jit(solution)/shard_map/ppermute | solution.py:26
  72.0 2.5 fusion.16
  74.5 1.2 select_maximum_fusion.2
  76.4 2.9 %fusion.1166 = (f32[3,8,32,255]{3,2,1,0:T(8,128)S(1)}, f32[3,8,32,255]{3,2,1,0:T(8,128)S(1)}, f32[3,8,32,255]{3,2,1,0:T(8,128)S(1)}, f32[3,8,32,255]{3,2,1,0:T(8...) fusion(f32[3,12,34,256]{3,2,1,0:T(8,128)S(1)} %get-tuple-elemen, ...), kind=kLoop, calls=%fused_computation.1893 | loop fusion | bytes 18800640 | tf_op jit(solution)/shard_map/slice | solution.py:68
  79.3 1.9 fusion.102
  83.8 1.0 fusion.189
  86.3 1.1 fusion.111
  87.4 1.0 fusion.171
  88.4 1.0 fusion.162
  90.4 1.1 fusion.135
  92.9 1.0 fusion.147
  93.9 1.0 fusion.106
  98.9 3.3 %multiply_add_fusion.2 = (f32[3,8,32,256]{3,2,1,0:T(8,128)S(1)}, f32[3,8,32,256]{3,2,1,0:T(8,128)}) fusion(f32[3,8,32,256]{3,2,1,0:T(8,128)S(1)} %multiply_add_fusion.3, f32[3,8,32,4]{3,2,1,0:T(8,128)S(1)} %copy-done.17, f32[8,32,256]{2,1,0:T(8,128)S(1)} %get-tuple-element.69, f32[3]{0:T(128)S(1)} %copy-done.74, f32[8,32,256]{2,1,0:T(8,128)S(1)} %get-tuple-element.119, ...), kind=kLoop, calls=%fused_computation.134 | loop fusion | flops 13565952 | bytes 12333416 | tf_op jit(solution)/shard_map/add | solution.py:141
  104.7 1.0 fusion.7
  106.0 2.7 fusion.2
  109.0 1.4 copy.491
  110.4 1.3 collective-permute-start.5
  111.7 3.0 %collective-permute-start.4 = (f32[3,2,32,256]{3,2,1,0:T(8,128)}, f32[3,2,32,256]{3,2,1,0:T(8,128)S(1)}, u32[]{:S(2)}, u32[]{:S(2)}) collective-permute-start(f32[3,2,32,256]{3,2,1,0:T(8,128)} %get-tuple-element.210), channel_id=1, source_target_pairs={{0,4},{4,8},{8,12},{12,16},{16,20},{20,24},{24,28},{1,5},{5,9},{9,... | collective-permute-start | bytes 589832 | tf_op jit(solution)/shard_map/ppermute | solution.py:26
  114.7 1.0 fusion.1133
  115.8 41.2 %psum.22 = f32[32,3,128]{2,0,1:T(8,128)S(1)} all-reduce(f32[32,3,128]{2,0,1:T(8,128)S(1)} %fusion.1133), channel_id=1, replica_groups=mesh['slab'=8,'split'=4] {'slab','split'}, use_global_device_ids=true, to_apply=%region_7.9 | all-reduce | flops 12288 | bytes 98304 | tf_op jit(solution)/shard_map/psum | solution.py:164
  157.1 1.3 gather_fusion.2
  158.8 2.9 %collective-permute-start.6 = (f32[3,12,2,256]{3,2,1,0:T(2,128)S(1)}, f32[3,12,2,256]{3,2,1,0:T(2,128)S(1)}, u32[]{:S(2)}, u32[]{:S(2)}) collective-permute-start(f32[3,12,2,256]{3,2,1,0:T(2,128)S(1)} %get-tuple-element.186), channel_id=1, source_target_pairs={{0,1},{1,2},{2,3},{4,5},{5,6},{6,7},{8,9},{9,10},{10,11},{12,13},{... | collective-permute-start | bytes 221192 | tf_op jit(solution)/shard_map/ppermute | solution.py:26
  161.8 4.2 %collective-permute-start.7 = (f32[3,12,2,256]{3,2,1,0:T(2,128)S(1)}, f32[3,12,2,256]{3,2,1,0:T(2,128)S(1)}, u32[]{:S(2)}, u32[]{:S(2)}) collective-permute-start(f32[3,12,2,256]{3,2,1,0:T(2,128)S(1)} %get-tuple-element.187), channel_id=1, source_target_pairs={{1,0},{2,1},{3,2},{5,4},{6,5},{7,6},{9,8},{10,9},{11,10},{13,12},{... | collective-permute-start | bytes 221192 | tf_op jit(solution)/shard_map/ppermute | solution.py:28
  167.7 1.0 fusion.148
  174.0 1.0 fusion.163
  177.8 1.2 fusion.172
  179.9 1.0 fusion.112
  181.0 1.0 fusion.190
  182.0 1.0 fusion.160
  184.3 1.0 fusion.108
  185.7 3.4 %multiply_add_fusion.1 = (f32[3,8,32,256]{3,2,1,0:T(8,128)S(1)}, f32[3,8,32,256]{3,2,1,0:T(8,128)}) fusion(f32[3,8,32,256]{3,2,1,0:T(8,128)S(1)} %get-tuple-element.31, f32[3,8,32,256]{3,2,1,0:T(8,128)S(1)} %copy-done.4, f32[3,8,32,4]{3,2,1,0:T(8,128)S(1)} %copy-done.18, f32[8,32,256]{2,1,0:T(8,128)S(1)} %get-tuple-element.67, f32[3]{0:T(128)S(1)} %copy-done.75, ...), kind=kLoop, calls=%fused_computation.133 | loop fusion | flops 13172736 | bytes 11546984 | tf_op jit(solution)/shard_map/add | solution.py:141
  189.0 1.0 slice_add_fusion
  190.8 1.1 fusion.1168
  192.0 1.3 copy.493
  193.3 1.0 copy.494
  195.8 1.8 fusion.8
  197.7 2.6 fusion.4
  200.7 1.4 copy.499
  202.1 1.3 collective-permute-start.9
  203.4 3.0 %collective-permute-start.8 = (f32[3,2,32,256]{3,2,1,0:T(8,128)}, f32[3,2,32,256]{3,2,1,0:T(8,128)S(1)}, u32[]{:S(2)}, u32[]{:S(2)}) collective-permute-start(f32[3,2,32,256]{3,2,1,0:T(8,128)} %get-tuple-element.203), channel_id=1, source_target_pairs={{0,4},{4,8},{8,12},{12,16},{16,20},{20,24},{24,28},{1,5},{5,9},{9,... | collective-permute-start | bytes 589832 | tf_op jit(solution)/shard_map/ppermute | solution.py:26
  206.4 1.7 fusion.1130
  208.1 39.7 %psum.23 = f32[32,3,128]{2,0,1:T(8,128)} all-reduce(f32[32,3,128]{2,0,1:T(8,128)} %fusion.1130), channel_id=1, replica_groups=mesh['slab'=8,'split'=4] {'slab','split'}, use_global_device_ids=true, to_apply=%region_11.13 | all-reduce | flops 12288 | bytes 98304 | tf_op jit(solution)/shard_map/psum | solution.py:164
  247.8 1.5 multiply_add_fusion.5
  249.3 3.7 %collective-permute-start.10 = (f32[3,12,2,256]{3,2,1,0:T(2,128)S(1)}, f32[3,12,2,256]{3,2,1,0:T(2,128)S(1)}, u32[]{:S(2)}, u32[]{:S(2)}) collective-permute-start(f32[3,12,2,256]{3,2,1,0:T(2,128)S(1)} %get-tuple-element.182), channel_id=1, source_target_pairs={{0,1},{1,2},{2,3},{4,5},{5,6},{6,7},{8,9},{9,10},{10,11},{12,13},{... | collective-permute-start | bytes 221192 | tf_op jit(solution)/shard_map/ppermute | solution.py:26
  253.0 3.3 %collective-permute-start.11 = (f32[3,12,2,256]{3,2,1,0:T(2,128)S(1)}, f32[3,12,2,256]{3,2,1,0:T(2,128)S(1)}, u32[]{:S(2)}, u32[]{:S(2)}) collective-permute-start(f32[3,12,2,256]{3,2,1,0:T(2,128)S(1)} %get-tuple-element.183), channel_id=1, source_target_pairs={{1,0},{2,1},{3,2},{5,4},{6,5},{7,6},{9,8},{10,9},{11,10},{13,12},{... | collective-permute-start | bytes 221192 | tf_op jit(solution)/shard_map/ppermute | solution.py:28
  258.1 1.0 fusion.149
  264.5 1.0 fusion.164
  268.3 1.3 fusion.173
  270.4 1.0 fusion.113
  271.4 1.0 fusion.191
  272.4 1.1 fusion.128
  273.5 1.0 fusion.161
  274.9 1.0 fusion.140
  276.2 3.4 %multiply_add_fusion = f32[3,8,32,256]{3,2,1,0:T(8,128)} fusion(f32[3,8,32,256]{3,2,1,0:T(8,128)S(1)} %copy-done.3, f32[3,8,32,4]{3,2,1,0:T(8,128)S(1)} %copy-done.16, f32[8,32,256]{2,1,0:T(8,128)S(1)} %get-tuple-element.89, f32[8,32,256]{2,1,0:T(8,128)S(1)} %get-tuple-element.121, f32[8,32,256]{2,1,0:T(8,128)S(1)} %get-tuple-element.65, ...), kind=kLoop, calls=%fused_computation.132 | loop fusion | flops 12582912 | bytes 9974120 | tf_op jit(solution)/shard_map/add | solution.py:163
  (461 shorter events, 49.1 us)
Async XLA Ops:
  0.6 6.9 %copy-start.73 = (s32[3,2,16]{2,1,0:T(2,128)S(1)}, s32[3,2,16]{2,1,0:T(2,128)}, u32[]{:S(2)}) copy-start(s32[3,2,16]{2,1,0:T(2,128)} %param.113) | copy-start | bytes 1156
  3.2 62.4 %collective-permute-start.1 = (f32[3,2,32,256]{3,2,1,0:T(8,128)}, f32[3,2,32,256]{3,2,1,0:T(8,128)S(1)}, u32[]{:S(2)}, u32[]{:S(2)}) collective-permute-start(f32[3,2,32,256]{3,2,1,0:T(8,128)} %get-tuple-element.218), channel_id=1, source_target_pairs={{4,0},{8,4},{12,8},{16,12},{20,16},{24,20},{28,24},{5,1},{9,5},{13... | collective-permute-start | bytes 589832 | tf_op jit(solution)/shard_map/ppermute | solution.py:28
  4.5 61.1 %collective-permute-start = (f32[3,2,32,256]{3,2,1,0:T(8,128)S(1)}, f32[3,2,32,256]{3,2,1,0:T(8,128)S(1)}, u32[]{:S(2)}, u32[]{:S(2)}) collective-permute-start(f32[3,2,32,256]{3,2,1,0:T(8,128)S(1)} %get-tuple-element.217), channel_id=1, source_target_pairs={{0,4},{4,8},{8,12},{12,16},{16,20},{20,24},{24,28},{1,5},{5,9},{9,... | collective-permute-start | bytes 589832 | tf_op jit(solution)/shard_map/ppermute | solution.py:26
  11.8 49.9 %copy-start.20 = (f32[32,3,128]{2,0,1:T(8,128)}, f32[32,3,128]{2,0,1:T(8,128)S(1)}, u32[]{:S(2)}) copy-start(f32[32,3,128]{2,0,1:T(8,128)S(1)} %multiply_add_fusion.8) | copy-start | bytes 147460
  15.6 2.3 copy-start.174
  15.6 2.3 copy-start.175
  15.8 3.9 %copy-start.72 = (f32[36]{0:T(128)S(1)}, f32[36]{0:T(128)}, u32[]{:S(2)}) copy-start(f32[36]{0:T(128)} %and_convert_fusion.4) | copy-start | bytes 436
  15.8 4.0 %copy-start.173 = (s32[16]{0:T(128)S(1)}, s32[16]{0:T(128)}, u32[]{:S(2)}) copy-start(s32[16]{0:T(128)} %get-tuple-element.220) | copy-start | bytes 196
  15.8 46.6 %copy-start.166 = (s32[16]{0:T(128)S(1)}, s32[16]{0:T(128)}, u32[]{:S(2)}) copy-start(s32[16]{0:T(128)} %get-tuple-element.222) | copy-start | bytes 196
  15.8 46.6 %copy-start.168 = (s32[16]{0:T(128)S(1)}, s32[16]{0:T(128)}, u32[]{:S(2)}) copy-start(s32[16]{0:T(128)} %get-tuple-element.230) | copy-start | bytes 196
  15.8 47.2 %copy-start.165 = (s32[16]{0:T(128)S(1)}, s32[16]{0:T(128)}, u32[]{:S(2)}) copy-start(s32[16]{0:T(128)} %get-tuple-element.226) | copy-start | bytes 196
  15.8 47.8 %copy-start.167 = (s32[16]{0:T(128)S(1)}, s32[16]{0:T(128)}, u32[]{:S(2)}) copy-start(s32[16]{0:T(128)} %get-tuple-element.24) | copy-start | bytes 196
  65.5 13.8 %copy-start.59 = (f32[8,32]{1,0:T(8,128)}, f32[8,32]{1,0:T(8,128)S(1)}, u32[]{:S(2)}) copy-start(f32[8,32]{1,0:T(8,128)S(1)} %get-tuple-element.247) | copy-start | bytes 3076
  65.5 18.3 %copy-start.47 = (f32[8,32]{1,0:T(8,128)}, f32[8,32]{1,0:T(8,128)S(1)}, u32[]{:S(2)}) copy-start(f32[8,32]{1,0:T(8,128)S(1)} %get-tuple-element.242) | copy-start | bytes 3076
  65.5 21.9 %copy-start.41 = (f32[8,32]{1,0:T(8,128)}, f32[8,32]{1,0:T(8,128)S(1)}, u32[]{:S(2)}) copy-start(f32[8,32]{1,0:T(8,128)S(1)} %get-tuple-element.240) | copy-start | bytes 3076
  65.5 22.9 %copy-start.56 = (f32[8,32]{1,0:T(8,128)}, f32[8,32]{1,0:T(8,128)S(1)}, u32[]{:S(2)}) copy-start(f32[8,32]{1,0:T(8,128)S(1)} %get-tuple-element.245) | copy-start | bytes 3076
  65.5 23.9 %copy-start.35 = (f32[8,32]{1,0:T(8,128)}, f32[8,32]{1,0:T(8,128)S(1)}, u32[]{:S(2)}) copy-start(f32[8,32]{1,0:T(8,128)S(1)} %get-tuple-element.243) | copy-start | bytes 3076
  65.5 24.9 %copy-start.53 = (f32[8,32]{1,0:T(8,128)}, f32[8,32]{1,0:T(8,128)S(1)}, u32[]{:S(2)}) copy-start(f32[8,32]{1,0:T(8,128)S(1)} %get-tuple-element.237) | copy-start | bytes 3076
  65.5 26.0 %copy-start.32 = (f32[8,32]{1,0:T(8,128)}, f32[8,32]{1,0:T(8,128)S(1)}, u32[]{:S(2)}) copy-start(f32[8,32]{1,0:T(8,128)S(1)} %get-tuple-element.238) | copy-start | bytes 3076
  65.5 27.0 %copy-start.26 = (f32[8,32]{1,0:T(8,128)}, f32[8,32]{1,0:T(8,128)S(1)}, u32[]{:S(2)}) copy-start(f32[8,32]{1,0:T(8,128)S(1)} %get-tuple-element.236) | copy-start | bytes 3076
  65.5 28.4 %copy-start.38 = (f32[8,32]{1,0:T(8,128)}, f32[8,32]{1,0:T(8,128)S(1)}, u32[]{:S(2)}) copy-start(f32[8,32]{1,0:T(8,128)S(1)} %get-tuple-element.239) | copy-start | bytes 3076
  65.5 29.4 %copy-start.29 = (f32[8,32]{1,0:T(8,128)}, f32[8,32]{1,0:T(8,128)S(1)}, u32[]{:S(2)}) copy-start(f32[8,32]{1,0:T(8,128)S(1)} %get-tuple-element.244) | copy-start | bytes 3076
  65.5 30.5 %copy-start.62 = (f32[8,32]{1,0:T(8,128)}, f32[8,32]{1,0:T(8,128)S(1)}, u32[]{:S(2)}) copy-start(f32[8,32]{1,0:T(8,128)S(1)} %get-tuple-element.246) | copy-start | bytes 3076
  65.6 31.3 %copy-start.44 = (f32[8,32]{1,0:T(8,128)}, f32[8,32]{1,0:T(8,128)S(1)}, u32[]{:S(2)}) copy-start(f32[8,32]{1,0:T(8,128)S(1)} %get-tuple-element.235) | copy-start | bytes 3076
  65.7 10.0 %collective-permute-start.3 = (f32[3,12,2,256]{3,2,1,0:T(2,128)S(1)}, f32[3,12,2,256]{3,2,1,0:T(2,128)S(1)}, u32[]{:S(2)}, u32[]{:S(2)}) collective-permute-start(f32[3,12,2,256]{3,2,1,0:T(2,128)S(1)} %get-tuple-element.190), channel_id=1, source_target_pairs={{1,0},{2,1},{3,2},{5,4},{6,5},{7,6},{9,8},{10,9},{11,10},{13,12},{... | collective-permute-start | bytes 221192 | tf_op jit(solution)/shard_map/ppermute | solution.py:28
  69.0 7.1 %collective-permute-start.2 = (f32[3,12,2,256]{3,2,1,0:T(2,128)S(1)}, f32[3,12,2,256]{3,2,1,0:T(2,128)S(1)}, u32[]{:S(2)}, u32[]{:S(2)}) collective-permute-start(f32[3,12,2,256]{3,2,1,0:T(2,128)S(1)} %get-tuple-element.191), channel_id=1, source_target_pairs={{0,1},{1,2},{2,3},{4,5},{5,6},{6,7},{8,9},{9,10},{10,11},{12,13},{... | collective-permute-start | bytes 221192 | tf_op jit(solution)/shard_map/ppermute | solution.py:26
  76.4 2.9 %copy-start.1 = (s32[4,8,32,256]{3,2,1,0:T(8,128)S(1)}, s32[4,8,32,256]{3,2,1,0:T(8,128)}, u32[]{:S(2)}) copy-start(s32[4,8,32,256]{3,2,1,0:T(8,128)} %param.109) | copy-start | bytes 3145732
  79.3 1.9 copy-start.11
  97.1 1.5 copy-start.17
  97.1 1.5 copy-start.74
  97.1 1.5 copy-start.77
  97.1 1.5 copy-start.80
  97.2 1.4 copy-start.83
  97.2 1.4 copy-start.86
  97.2 1.4 copy-start.89
  97.2 1.4 copy-start.92
  97.2 1.4 copy-start.95
  97.2 1.4 copy-start.98
  97.2 1.4 copy-start.101
  97.2 1.4 copy-start.104
  97.3 1.4 copy-start.107
  97.3 1.4 copy-start.110
  97.3 1.4 copy-start.113
  97.3 1.4 copy-start.116
  102.2 2.5 copy-start.164
  102.2 2.6 copy-start.24
  105.8 2.9 %copy-start.171 = (f32[16]{0:T(128)S(1)}, f32[16]{0:T(128)}, u32[]{:S(2)}) copy-start(f32[16]{0:T(128)} %get-tuple-element.231) | copy-start | bytes 196
  105.8 2.9 %copy-start.172 = (s32[16]{0:T(128)S(1)}, s32[16]{0:T(128)}, u32[]{:S(2)}) copy-start(s32[16]{0:T(128)} %get-tuple-element.223) | copy-start | bytes 196
  106.0 51.0 %copy-start.21 = (f32[32,3,128]{2,0,1:T(8,128)S(1)}, f32[32,3,128]{2,0,1:T(8,128)}, u32[]{:S(2)}) copy-start(f32[32,3,128]{2,0,1:T(8,128)} %copy-done.20) | copy-start | bytes 147460
  106.0 51.0 %copy-start.22 = (f32[32,3,128]{2,0,1:T(8,128)S(1)}, f32[32,3,128]{2,0,1:T(8,128)}, u32[]{:S(2)}) copy-start(f32[32,3,128]{2,0,1:T(8,128)} %get-tuple-element.30) | copy-start | bytes 147460
  110.4 48.3 %collective-permute-start.5 = (f32[3,2,32,256]{3,2,1,0:T(8,128)}, f32[3,2,32,256]{3,2,1,0:T(8,128)S(1)}, u32[]{:S(2)}, u32[]{:S(2)}) collective-permute-start(f32[3,2,32,256]{3,2,1,0:T(8,128)} %get-tuple-element.211), channel_id=1, source_target_pairs={{4,0},{8,4},{12,8},{16,12},{20,16},{24,20},{28,24},{5,1},{9,5},{13... | collective-permute-start | bytes 589832 | tf_op jit(solution)/shard_map/ppermute | solution.py:28
  111.7 47.1 %collective-permute-start.4 = (f32[3,2,32,256]{3,2,1,0:T(8,128)}, f32[3,2,32,256]{3,2,1,0:T(8,128)S(1)}, u32[]{:S(2)}, u32[]{:S(2)}) collective-permute-start(f32[3,2,32,256]{3,2,1,0:T(8,128)} %get-tuple-element.210), channel_id=1, source_target_pairs={{0,4},{4,8},{8,12},{12,16},{16,20},{20,24},{24,28},{1,5},{5,9},{9,... | collective-permute-start | bytes 589832 | tf_op jit(solution)/shard_map/ppermute | solution.py:26
  157.0 9.7 %copy-start.23 = (f32[32,3,128]{2,0,1:T(8,128)}, f32[32,3,128]{2,0,1:T(8,128)S(1)}, u32[]{:S(2)}) copy-start(f32[32,3,128]{2,0,1:T(8,128)S(1)} %psum.22) | copy-start | bytes 147460
  157.1 1.7 copy-start.52
  158.8 14.0 %collective-permute-start.6 = (f32[3,12,2,256]{3,2,1,0:T(2,128)S(1)}, f32[3,12,2,256]{3,2,1,0:T(2,128)S(1)}, u32[]{:S(2)}, u32[]{:S(2)}) collective-permute-start(f32[3,12,2,256]{3,2,1,0:T(2,128)S(1)} %get-tuple-element.186), channel_id=1, source_target_pairs={{0,1},{1,2},{2,3},{4,5},{5,6},{6,7},{8,9},{9,10},{10,11},{12,13},{... | collective-permute-start | bytes 221192 | tf_op jit(solution)/shard_map/ppermute | solution.py:26
  161.8 11.0 %collective-permute-start.7 = (f32[3,12,2,256]{3,2,1,0:T(2,128)S(1)}, f32[3,12,2,256]{3,2,1,0:T(2,128)S(1)}, u32[]{:S(2)}, u32[]{:S(2)}) collective-permute-start(f32[3,12,2,256]{3,2,1,0:T(2,128)S(1)} %get-tuple-element.187), channel_id=1, source_target_pairs={{1,0},{2,1},{3,2},{5,4},{6,5},{7,6},{9,8},{10,9},{11,10},{13,12},{... | collective-permute-start | bytes 221192 | tf_op jit(solution)/shard_map/ppermute | solution.py:28
  189.0 85.4 %copy-start = (f32[3,8,32,256]{3,2,1,0:T(8,128)}, f32[3,8,32,256]{3,2,1,0:T(8,128)S(1)}, u32[]{:S(2)}) copy-start(f32[3,8,32,256]{3,2,1,0:T(8,128)S(1)} %get-tuple-element.25) | copy-start | bytes 2359300
  195.7 2.0 copy-start.25
  197.5 2.8 %copy-start.169 = (f32[16]{0:T(128)S(1)}, f32[16]{0:T(128)}, u32[]{:S(2)}) copy-start(f32[16]{0:T(128)} %get-tuple-element.228) | copy-start | bytes 196
  197.5 2.8 %copy-start.170 = (s32[16]{0:T(128)S(1)}, s32[16]{0:T(128)}, u32[]{:S(2)}) copy-start(s32[16]{0:T(128)} %get-tuple-element.227) | copy-start | bytes 196
  202.1 47.1 %collective-permute-start.9 = (f32[3,2,32,256]{3,2,1,0:T(8,128)}, f32[3,2,32,256]{3,2,1,0:T(8,128)S(1)}, u32[]{:S(2)}, u32[]{:S(2)}) collective-permute-start(f32[3,2,32,256]{3,2,1,0:T(8,128)} %get-tuple-element.204), channel_id=1, source_target_pairs={{4,0},{8,4},{12,8},{16,12},{20,16},{24,20},{28,24},{5,1},{9,5},{13... | collective-permute-start | bytes 589832 | tf_op jit(solution)/shard_map/ppermute | solution.py:28
  203.4 45.9 %collective-permute-start.8 = (f32[3,2,32,256]{3,2,1,0:T(8,128)}, f32[3,2,32,256]{3,2,1,0:T(8,128)S(1)}, u32[]{:S(2)}, u32[]{:S(2)}) collective-permute-start(f32[3,2,32,256]{3,2,1,0:T(8,128)} %get-tuple-element.203), channel_id=1, source_target_pairs={{0,4},{4,8},{8,12},{12,16},{16,20},{20,24},{24,28},{1,5},{5,9},{9,... | collective-permute-start | bytes 589832 | tf_op jit(solution)/shard_map/ppermute | solution.py:26
  249.3 13.9 %collective-permute-start.10 = (f32[3,12,2,256]{3,2,1,0:T(2,128)S(1)}, f32[3,12,2,256]{3,2,1,0:T(2,128)S(1)}, u32[]{:S(2)}, u32[]{:S(2)}) collective-permute-start(f32[3,12,2,256]{3,2,1,0:T(2,128)S(1)} %get-tuple-element.182), channel_id=1, source_target_pairs={{0,1},{1,2},{2,3},{4,5},{5,6},{6,7},{8,9},{9,10},{10,11},{12,13},{... | collective-permute-start | bytes 221192 | tf_op jit(solution)/shard_map/ppermute | solution.py:26
  253.0 10.2 %collective-permute-start.11 = (f32[3,12,2,256]{3,2,1,0:T(2,128)S(1)}, f32[3,12,2,256]{3,2,1,0:T(2,128)S(1)}, u32[]{:S(2)}, u32[]{:S(2)}) collective-permute-start(f32[3,12,2,256]{3,2,1,0:T(2,128)S(1)} %get-tuple-element.183), channel_id=1, source_target_pairs={{1,0},{2,1},{3,2},{5,4},{6,5},{7,6},{9,8},{10,9},{11,10},{13,12},{... | collective-permute-start | bytes 221192 | tf_op jit(solution)/shard_map/ppermute | solution.py:28
  (124 other events, 155.4 us)
where the time goes:
time: 285 us; the launch traced here: 280 us
  blocking collectives  123 us (43%)
  other arithmetic  86.3 us (30%)
  starting transfers between devices  33.4 us (12%)
  local copies, waits for them, and re-layouts  29.6 us (10%)
  between operations  4.09 us (1%)
  matrix products  3.59 us (1%)
    psum x3, blocking collectives, per_device(): particle_force = lax.psum(particle_local, ('slab', 'split'))  123 us
    mul x49, other arithmetic, add_bond(): return bond_total + direction[:, None, None, None] * coefficient[None]  47.1 us
    ppermute x6, starting transfers between devices, with_halo(): lax.ppermute(tail, axis, [(i, (i + 1) % count) for i in range(ends)])  18.8 us
    ppermute x6, starting transfers between devices, with_halo(): lax.ppermute(head, axis, [((i + 1) % count, i) for i in range(ends)])  14.6 us
    add x3, other arithmetic, per_device(): displacement = displacement + time_step * half_velocity  8.5 us
    slice x7, local copies, waits for them, and re-layouts, shift_depth(): return jnp.concatenate([filler, values_in[..., :shift_size]], axis=-1)  8.44 us
    reduce_sum x3, other arithmetic, contact_tile(): return (jnp.sum(pulled, axis=2), -jnp.sum(pulled, axis=1))  7.3 us
    concatenate x10, other arithmetic, with_halo(): jnp.concatenate([lax.ppermute(tail, axis, [(i, (i + 1) % count) for i in...  6.48 us
  transfers between devices with their start and end apart: 12, of which 1 were waited for; matrix products, arithmetic and copies ran while one was open for 14% of the time, Pallas kernels for 0%

commit v1 on v0

--- a/solution.py
+++ b/solution.py
@@ -3,6 +3,7 @@
 import jax.numpy as jnp
 from jax import lax
 from jax.sharding import PartitionSpec as P
+from jax.lax import all_gather
 
 SUB = 3
 SL = 4
@@ -161,7 +162,11 @@
         )
         acceleration = forces
         velocity = half_velocity + 0.5 * time_step * acceleration
-        particle_force = lax.psum(particle_local, ("slab", "split"))
+
+        def choose_the_hubs(across, local_values):
+            return jnp.sum(all_gather(local_values, across), 0)
+
+        particle_force = choose_the_hubs(("slab", "split"), particle_local)
         proj_acc = inverse_mass * particle_force
         proj_vel = proj_half + 0.5 * time_step * proj_acc
     return (displacement, velocity, proj_pos, proj_vel)

time: 285 us -> 270 us (0.947)
  the two profiles are of different devices: /device:TPU:4 before, /device:TPU:0 now
where the time goes in v1:
time: 270 us; the launch traced here: 265 us
  other arithmetic  123 us (46%)
  waiting for transfers between devices  56.9 us (21%)
  starting transfers between devices  33.9 us (13%)
  local copies, waits for them, and re-layouts  32.1 us (12%)
  between operations  16.4 us (6%)
  matrix products  3.32 us (1%)
    mul x49, other arithmetic, add_bond(): return bond_total + direction[:, None, None, None] * coefficient[None]  71.6 us
    all_gather x3, waiting for transfers between devices, choose_the_hubs(): return jnp.sum(all_gather(local_values, across), 0)  56.8 us
    ppermute x6, starting transfers between devices, with_halo(): lax.ppermute(tail, axis, [(i, (i + 1) % count) for i in range(ends)])  25.6 us
    slice x7, local copies, waits for them, and re-layouts, shift_depth(): return jnp.concatenate([filler, values_in[..., :shift_size]], axis=-1)  11.1 us
    add x3, other arithmetic, per_device(): displacement = displacement + time_step * half_velocity  11.1 us
    ppermute x6, starting transfers between devices, with_halo(): lax.ppermute(head, axis, [((i + 1) % count, i) for i in range(ends)])  8.11 us
    reduce_sum x3, other arithmetic, contact_tile(): return (jnp.sum(pulled, axis=2), -jnp.sum(pulled, axis=1))  7.34 us
    add x1, other arithmetic, per_device(): velocity = half_velocity + 0.5 * time_step * acceleration  6.91 us
  transfers between devices with their start and end apart: 15, of which 2 were waited for; matrix products, arithmetic and copies ran while one was open for 46% of the time, Pallas kernels for 0%

profile of v1, /device:TPU:0, one launch (start us, length us, event | category | flops | bytes accessed | tf_op | source)
XLA Modules:
  0.0 265.5 jit_solution(9253597896889141393)
XLA Ops:
  7.3 1.8 multiply_add_fusion.3
  11.1 3.0 %collective-permute-start = (f32[3,2,32,256]{3,2,1,0:T(8,128)S(1)}, f32[3,2,32,256]{3,2,1,0:T(8,128)S(1)}, u32[]{:S(2)}, u32[]{:S(2)}) collective-permute-start(f32[3,2,32,256]{3,2,1,0:T(8,128)S(1)} %get-tuple-element.217), channel_id=1, source_target_pairs={{0,4},{4,8},{8,12},{12,16},{16,20},{20,24},{24,28},{1,5},{5,9},{9,... | collective-permute-start | bytes 589832 | tf_op jit(solution)/shard_map/ppermute | solution.py:27
  19.3 2.0 fusion
  23.6 1.5 fusion.1172
  25.4 1.4 copy.495
  31.4 6.0 %collective-permute-start.2 = (f32[3,12,2,256]{3,2,1,0:T(2,128)S(1)}, f32[3,12,2,256]{3,2,1,0:T(2,128)S(1)}, u32[]{:S(2)}, u32[]{:S(2)}) collective-permute-start(f32[3,12,2,256]{3,2,1,0:T(2,128)S(1)} %get-tuple-element.191), channel_id=1, source_target_pairs={{0,1},{1,2},{2,3},{4,5},{5,6},{6,7},{8,9},{9,10},{10,11},{12,13},{... | collective-permute-start | bytes 221192 | tf_op jit(solution)/shard_map/ppermute | solution.py:27
  37.4 2.5 fusion.16
  41.4 2.6 fusion.1166
  62.5 3.3 %multiply_add_fusion.2 = (f32[3,8,32,256]{3,2,1,0:T(8,128)S(1)}, f32[3,8,32,256]{3,2,1,0:T(8,128)}) fusion(f32[3,8,32,256]{3,2,1,0:T(8,128)S(1)} %multiply_add_fusion.3, f32[3,8,32,4]{3,2,1,0:T(8,128)S(1)} %copy-done.45, f32[8,32,256]{2,1,0:T(8,128)S(1)} %get-tuple-element.69, f32[3]{0:T(128)S(1)} %copy-done.113, f32[8,32,256]{2,1,0:T(8,128)S(1)} %get-tuple-element.119, ...), kind=kLoop, calls=%fused_computation.134 | loop fusion | flops 13565952 | bytes 12333416 | tf_op jit(solution)/shard_map/add | solution.py:142
  66.7 1.4 fusion.1170
  70.8 3.7 %collective-permute-start.4 = (f32[3,2,32,256]{3,2,1,0:T(8,128)S(1)}, f32[3,2,32,256]{3,2,1,0:T(8,128)S(1)}, u32[]{:S(2)}, u32[]{:S(2)}) collective-permute-start(f32[3,2,32,256]{3,2,1,0:T(8,128)S(1)} %get-tuple-element.210), channel_id=1, source_target_pairs={{0,4},{4,8},{8,12},{12,16},{16,20},{20,24},{24,28},{1,5},{5,9},{9,... | collective-permute-start | bytes 589832 | tf_op jit(solution)/shard_map/ppermute | solution.py:27
  74.6 1.4 gather_fusion.4
  76.8 4.3 %collective-permute-start.6 = (f32[3,12,2,256]{3,2,1,0:T(2,128)S(1)}, f32[3,12,2,256]{3,2,1,0:T(2,128)S(1)}, u32[]{:S(2)}, u32[]{:S(2)}) collective-permute-start(f32[3,12,2,256]{3,2,1,0:T(2,128)S(1)} %get-tuple-element.186), channel_id=1, source_target_pairs={{0,1},{1,2},{2,3},{4,5},{5,6},{6,7},{8,9},{9,10},{10,11},{12,13},{... | collective-permute-start | bytes 221192 | tf_op jit(solution)/shard_map/ppermute | solution.py:27
  81.1 1.5 collective-permute-start.7
  83.4 1.7 fusion.181
  85.1 1.8 fusion.148
  87.5 1.7 fusion.118
  89.2 1.7 fusion.184
  90.9 1.6 fusion.103
  92.5 1.6 fusion.154
  96.2 1.7 fusion.178
  97.9 1.6 fusion.130
  99.5 1.7 fusion.160
  101.2 1.7 fusion.139
  102.9 2.1 fusion.190
  105.1 1.7 fusion.136
  106.8 1.7 fusion.108
  108.5 1.8 fusion.172
  110.3 1.8 fusion.112
  112.1 1.8 fusion.163
  113.9 1.5 reduce_sum.111
  118.1 2.7 %fusion.2 = (f32[16,3,128]{2,1,0:T(4,128)}, f32[16,3,128]{2,1,0:T(4,128)S(1)}) fusion(f32[16,128,128]{2,1,0:T(8,128)S(1)} %exponential_multiply_fusion.1, f32[16,3,128]{2,1,0:T(4,128)S(1)} %gather_fusion.1, f32[16,3,128]{2,1,0:T(4,128)S(1)} %broadcast_select_fusion.1), kind=kLoop, calls=%fused_computation.14 | loop fusion | flops 3133440 | bytes 1146880 | tf_op jit(solution)/shard_map/vmap()/reduce_sum | solution.py:101
  121.1 1.4 copy.503
  122.4 6.0 %multiply_add_fusion.1 = (f32[3,8,32,256]{3,2,1,0:T(8,128)S(1)}, f32[3,8,32,256]{3,2,1,0:T(8,128)}) fusion(f32[3,8,32,256]{3,2,1,0:T(8,128)S(1)} %get-tuple-element.31, f32[3,8,32,256]{3,2,1,0:T(8,128)} %get-tuple-element.32, f32[3,8,32,4]{3,2,1,0:T(8,128)} %copy.503, f32[8,32,256]{2,1,0:T(8,128)} %get-tuple-element.67, f32[3]{0:T(128)} %constant.1031.clone, ...), kind=kLoop, calls=%fused_computation.133 | loop fusion | flops 13172736 | bytes 11546984 | tf_op jit(solution)/shard_map/add | solution.py:142
  128.7 1.5 fusion.1168
  133.2 4.4 %collective-permute-start.8 = (f32[3,2,32,256]{3,2,1,0:T(8,128)S(1)}, f32[3,2,32,256]{3,2,1,0:T(8,128)S(1)}, u32[]{:S(2)}, u32[]{:S(2)}) collective-permute-start(f32[3,2,32,256]{3,2,1,0:T(8,128)S(1)} %get-tuple-element.203), channel_id=1, source_target_pairs={{0,4},{4,8},{8,12},{12,16},{16,20},{20,24},{24,28},{1,5},{5,9},{9,... | collective-permute-start | bytes 589832 | tf_op jit(solution)/shard_map/ppermute | solution.py:27
  139.1 4.3 %collective-permute-start.10 = (f32[3,12,2,256]{3,2,1,0:T(2,128)S(1)}, f32[3,12,2,256]{3,2,1,0:T(2,128)S(1)}, u32[]{:S(2)}, u32[]{:S(2)}) collective-permute-start(f32[3,12,2,256]{3,2,1,0:T(2,128)S(1)} %get-tuple-element.182), channel_id=1, source_target_pairs={{0,1},{1,2},{2,3},{4,5},{5,6},{6,7},{8,9},{9,10},{10,11},{12,13},{... | collective-permute-start | bytes 221192 | tf_op jit(solution)/shard_map/ppermute | solution.py:27
  143.4 1.5 collective-permute-start.11
  145.6 1.7 fusion.182
  147.3 1.8 fusion.149
  149.1 1.6 fusion.104
  151.0 1.7 fusion.119
  152.7 1.7 fusion.185
  154.4 1.6 fusion.155
  156.3 2.1 fusion.1162
  158.5 1.7 fusion.179
  160.1 2.4 fusion.1163
  162.5 1.7 fusion.161
  164.2 1.7 fusion.140
  165.9 25.1 %all-gather.9.cloned.1.call-done = f32[1024,3,128]{2,0,1:T(8,128)} async-done(((f32[32,3,128]{2,0,1:T(8,128)}), f32[1024,3,128]{2,0,1:T(8,128)}) %all-gather.9.cloned.1.call-update) | async-done | bytes 1572880 | tf_op jit(solution)/shard_map/all_gather | solution.py:167
  191.1 2.1 reduce_sum.115
  195.3 1.5 gather_fusion.2
  196.8 2.0 fusion.8
  199.0 2.7 %fusion.4 = (f32[16,3,128]{2,1,0:T(4,128)S(1)}, f32[16,3,128]{2,1,0:T(4,128)}) fusion(f32[16,128,128]{2,1,0:T(8,128)S(1)} %exponential_multiply_fusion, f32[16,3,128]{2,1,0:T(4,128)S(1)} %gather_fusion.2, f32[16,3,128]{2,1,0:T(4,128)S(1)} %copy-done.57), kind=kLoop, calls=%fused_computation.16 | loop fusion | flops 3133440 | bytes 1146880 | tf_op jit(solution)/shard_map/vmap()/reduce_sum | solution.py:101
  202.7 2.9 %fusion.131 = (f32[8,32,256]{2,1,0:T(8,128)}, f32[8,32,256]{2,1,0:T(8,128)}) fusion(f32[3,12,34,256]{3,2,1,0:T(8,128)S(1)} %get-tuple-element.181, f32[8,32]{1,0:T(8,128)S(1)} %copy-done.63, f32[256]{0:T(256)S(1)} %copy-done.54, f32[3,8,32,256]{3,2,1,0:T(8,128)S(1)} %get-tuple-element.25, pred[1,8,32,256]{3,2,1,0:T(8,128)(4,1)} %copy-done.4, ...), kind=kLoop, calls=%fused_computation.696 | loop fusion | flops 4325376 | bytes 3276800 | tf_op jit(solution)/shard_map/mul | solution.py:60
  205.8 1.7 fusion.191
  207.5 1.8 fusion.137
  209.4 1.8 fusion.128
  211.2 1.7 fusion.173
  213.0 1.8 fusion.113
  215.0 1.8 fusion.164
  217.9 6.9 %multiply_add_fusion = f32[3,8,32,256]{3,2,1,0:T(8,128)} fusion(f32[3,8,32,256]{3,2,1,0:T(8,128)} %get-tuple-element.26, f32[3,8,32,4]{3,2,1,0:T(8,128)S(1)} %copy.511, f32[8,32,256]{2,1,0:T(8,128)} %get-tuple-element.89, f32[8,32,256]{2,1,0:T(8,128)} %get-tuple-element.121, f32[8,32,256]{2,1,0:T(8,128)} %get-tuple-element.65, ...), kind=kLoop, calls=%fused_computation.132 | loop fusion | flops 12582912 | bytes 9974120 | tf_op jit(solution)/shard_map/add | solution.py:164
  224.9 31.7 %all-gather.11.cloned.1.call-done = f32[1024,3,128]{2,0,1:T(8,128)} async-done(((f32[32,3,128]{2,0,1:T(8,128)}), f32[1024,3,128]{2,0,1:T(8,128)}) %all-gather.11.cloned.1.call-update) | async-done | bytes 1572880 | tf_op jit(solution)/shard_map/all_gather | solution.py:167
  256.6 1.5 reduce_sum.119
  (462 shorter events, 55.5 us)
Async XLA Ops:
  7.2 7.0 %copy-start.112 = (s32[3,2,16]{2,1,0:T(2,128)S(1)}, s32[3,2,16]{2,1,0:T(2,128)}, u32[]{:S(2)}) copy-start(s32[3,2,16]{2,1,0:T(2,128)} %param.113) | copy-start | bytes 1156
  7.2 8.2 %copy-start.103 = (f32[32,3,128]{2,0,1:T(8,128)S(1)}, f32[32,3,128]{2,0,1:T(8,128)}, u32[]{:S(2)}) copy-start(f32[32,3,128]{2,0,1:T(8,128)} %param.110) | copy-start | bytes 147460
  7.2 8.2 %copy-start.86 = (f32[32,3,128]{2,0,1:T(8,128)S(1)}, f32[32,3,128]{2,0,1:T(8,128)}, u32[]{:S(2)}) copy-start(f32[32,3,128]{2,0,1:T(8,128)} %param.111) | copy-start | bytes 147460
  7.2 8.2 %copy-start.88 = (f32[32,3,128]{2,0,1:T(8,128)S(1)}, f32[32,3,128]{2,0,1:T(8,128)}, u32[]{:S(2)}) copy-start(f32[32,3,128]{2,0,1:T(8,128)} %param.112) | copy-start | bytes 147460
  7.2 106.6 %all-gather.7.cloned.1.call-start = ((), (), s32[]{:S(2)}) async-start(), calls=%async_computation | async-start | bytes 1622016 | tf_op jit(solution)/shard_map/all_gather | solution.py:167
  9.8 20.3 %collective-permute-start.1 = (f32[3,2,32,256]{3,2,1,0:T(8,128)}, f32[3,2,32,256]{3,2,1,0:T(8,128)S(1)}, u32[]{:S(2)}, u32[]{:S(2)}) collective-permute-start(f32[3,2,32,256]{3,2,1,0:T(8,128)} %get-tuple-element.218), channel_id=1, source_target_pairs={{4,0},{8,4},{12,8},{16,12},{20,16},{24,20},{28,24},{5,1},{9,5},{13... | collective-permute-start | bytes 589832 | tf_op jit(solution)/shard_map/ppermute | solution.py:29
  11.1 19.0 %collective-permute-start = (f32[3,2,32,256]{3,2,1,0:T(8,128)S(1)}, f32[3,2,32,256]{3,2,1,0:T(8,128)S(1)}, u32[]{:S(2)}, u32[]{:S(2)}) collective-permute-start(f32[3,2,32,256]{3,2,1,0:T(8,128)S(1)} %get-tuple-element.217), channel_id=1, source_target_pairs={{0,4},{4,8},{8,12},{12,16},{16,20},{20,24},{24,28},{1,5},{5,9},{9,... | collective-permute-start | bytes 589832 | tf_op jit(solution)/shard_map/ppermute | solution.py:27
  22.3 168.7 %all-gather.9.cloned.1.call-start = ((), (), s32[]{:S(2)}) async-start(), calls=%async_computation.1 | async-start | bytes 1622016 | tf_op jit(solution)/shard_map/all_gather | solution.py:167
  23.0 135.5 %copy-start.53 = (f32[256]{0:T(256)}, f32[256]{0:T(256)S(1)}, u32[]{:S(2)}) copy-start(f32[256]{0:T(256)S(1)} %get-tuple-element.265) | copy-start | bytes 3076
  23.0 141.2 %copy-start.51 = (f32[256]{0:T(256)}, f32[256]{0:T(256)S(1)}, u32[]{:S(2)}) copy-start(f32[256]{0:T(256)S(1)} %and_convert_fusion.2) | copy-start | bytes 3076
  23.6 140.7 %copy-start.49 = (f32[256]{0:T(256)}, f32[256]{0:T(256)S(1)}, u32[]{:S(2)}) copy-start(f32[256]{0:T(256)S(1)} %get-tuple-element.267) | copy-start | bytes 3076
  23.6 3.9 %copy-start.160 = (s32[16]{0:T(128)S(1)}, s32[16]{0:T(128)}, u32[]{:S(2)}) copy-start(s32[16]{0:T(128)} %get-tuple-element.230) | copy-start | bytes 196
  30.0 14.0 %copy-start.100 = (f32[8,32]{1,0:T(8,128)}, f32[8,32]{1,0:T(8,128)S(1)}, u32[]{:S(2)}) copy-start(f32[8,32]{1,0:T(8,128)S(1)} %get-tuple-element.247) | copy-start | bytes 3076
  30.0 17.4 %copy-start.82 = (f32[8,32]{1,0:T(8,128)}, f32[8,32]{1,0:T(8,128)S(1)}, u32[]{:S(2)}) copy-start(f32[8,32]{1,0:T(8,128)S(1)} %get-tuple-element.242) | copy-start | bytes 3076
  30.0 21.1 %copy-start.71 = (f32[8,32]{1,0:T(8,128)}, f32[8,32]{1,0:T(8,128)S(1)}, u32[]{:S(2)}) copy-start(f32[8,32]{1,0:T(8,128)S(1)} %get-tuple-element.240) | copy-start | bytes 3076
  30.0 23.1 %copy-start.64 = (f32[8,32]{1,0:T(8,128)}, f32[8,32]{1,0:T(8,128)S(1)}, u32[]{:S(2)}) copy-start(f32[8,32]{1,0:T(8,128)S(1)} %get-tuple-element.243) | copy-start | bytes 3076
  30.0 25.2 %copy-start.75 = (f32[8,32]{1,0:T(8,128)}, f32[8,32]{1,0:T(8,128)S(1)}, u32[]{:S(2)}) copy-start(f32[8,32]{1,0:T(8,128)S(1)} %get-tuple-element.238) | copy-start | bytes 3076
  30.0 26.2 %copy-start.58 = (f32[8,32]{1,0:T(8,128)}, f32[8,32]{1,0:T(8,128)S(1)}, u32[]{:S(2)}) copy-start(f32[8,32]{1,0:T(8,128)S(1)} %get-tuple-element.236) | copy-start | bytes 3076
  30.0 27.5 %copy-start.68 = (f32[8,32]{1,0:T(8,128)}, f32[8,32]{1,0:T(8,128)S(1)}, u32[]{:S(2)}) copy-start(f32[8,32]{1,0:T(8,128)S(1)} %get-tuple-element.239) | copy-start | bytes 3076
  30.0 28.6 %copy-start.61 = (f32[8,32]{1,0:T(8,128)}, f32[8,32]{1,0:T(8,128)S(1)}, u32[]{:S(2)}) copy-start(f32[8,32]{1,0:T(8,128)S(1)} %get-tuple-element.244) | copy-start | bytes 3076
  30.0 30.6 %copy-start.79 = (f32[8,32]{1,0:T(8,128)}, f32[8,32]{1,0:T(8,128)S(1)}, u32[]{:S(2)}) copy-start(f32[8,32]{1,0:T(8,128)S(1)} %get-tuple-element.235) | copy-start | bytes 3076
  30.0 11.1 %copy-start.20 = (f32[3,2,32,256]{3,2,1,0:T(8,128)}, f32[3,2,32,256]{3,2,1,0:T(8,128)S(1)}, u32[]{:S(2)}) copy-start(f32[3,2,32,256]{3,2,1,0:T(8,128)S(1)} %collective-permute-done.1) | copy-start | bytes 589828
  30.1 11.0 %collective-permute-start.3 = (f32[3,12,2,256]{3,2,1,0:T(2,128)S(1)}, f32[3,12,2,256]{3,2,1,0:T(2,128)S(1)}, u32[]{:S(2)}, u32[]{:S(2)}) collective-permute-start(f32[3,12,2,256]{3,2,1,0:T(2,128)S(1)} %get-tuple-element.190), channel_id=1, source_target_pairs={{1,0},{2,1},{3,2},{5,4},{6,5},{7,6},{9,8},{10,9},{11,10},{13,12},{... | collective-permute-start | bytes 221192 | tf_op jit(solution)/shard_map/ppermute | solution.py:29
  31.4 9.7 %collective-permute-start.2 = (f32[3,12,2,256]{3,2,1,0:T(2,128)S(1)}, f32[3,12,2,256]{3,2,1,0:T(2,128)S(1)}, u32[]{:S(2)}, u32[]{:S(2)}) collective-permute-start(f32[3,12,2,256]{3,2,1,0:T(2,128)S(1)} %get-tuple-element.191), channel_id=1, source_target_pairs={{0,1},{1,2},{2,3},{4,5},{5,6},{6,7},{8,9},{9,10},{10,11},{12,13},{... | collective-permute-start | bytes 221192 | tf_op jit(solution)/shard_map/ppermute | solution.py:27
  45.8 106.9 %copy-start.7 = (pred[1,8,32,256]{3,2,1,0:T(8,128)(4,1)}, pred[1,8,32,256]{3,2,1,0:T(8,128)(4,1)S(1)}, u32[]{:S(2)}) copy-start(pred[1,8,32,256]{3,2,1,0:T(8,128)(4,1)S(1)} %get-tuple-element.48) | copy-start | bytes 196612
  47.3 99.9 %copy-start.4 = (pred[1,8,32,256]{3,2,1,0:T(8,128)(4,1)}, pred[1,8,32,256]{3,2,1,0:T(8,128)(4,1)S(1)}, u32[]{:S(2)}) copy-start(pred[1,8,32,256]{3,2,1,0:T(8,128)(4,1)S(1)} %get-tuple-element.38) | copy-start | bytes 196612
  49.7 97.6 %copy-start.15 = (pred[1,8,32,256]{3,2,1,0:T(8,128)(4,1)}, pred[1,8,32,256]{3,2,1,0:T(8,128)(4,1)S(1)}, u32[]{:S(2)}) copy-start(pred[1,8,32,256]{3,2,1,0:T(8,128)(4,1)S(1)} %get-tuple-element.40) | copy-start | bytes 196612
  51.0 100.0 %copy-start.13 = (pred[1,8,32,256]{3,2,1,0:T(8,128)(4,1)}, pred[1,8,32,256]{3,2,1,0:T(8,128)(4,1)S(1)}, u32[]{:S(2)}) copy-start(pred[1,8,32,256]{3,2,1,0:T(8,128)(4,1)S(1)} %get-tuple-element.36) | copy-start | bytes 196612
  51.0 103.4 %copy-start.10 = (pred[1,8,32,256]{3,2,1,0:T(8,128)(4,1)}, pred[1,8,32,256]{3,2,1,0:T(8,128)(4,1)S(1)}, u32[]{:S(2)}) copy-start(pred[1,8,32,256]{3,2,1,0:T(8,128)(4,1)S(1)} %get-tuple-element.141) | copy-start | bytes 196612
  69.6 7.2 %collective-permute-start.5 = (f32[3,2,32,256]{3,2,1,0:T(8,128)}, f32[3,2,32,256]{3,2,1,0:T(8,128)S(1)}, u32[]{:S(2)}, u32[]{:S(2)}) collective-permute-start(f32[3,2,32,256]{3,2,1,0:T(8,128)} %get-tuple-element.211), channel_id=1, source_target_pairs={{4,0},{8,4},{12,8},{16,12},{20,16},{24,20},{28,24},{5,1},{9,5},{13... | collective-permute-start | bytes 589832 | tf_op jit(solution)/shard_map/ppermute | solution.py:29
  70.8 5.9 %collective-permute-start.4 = (f32[3,2,32,256]{3,2,1,0:T(8,128)S(1)}, f32[3,2,32,256]{3,2,1,0:T(8,128)S(1)}, u32[]{:S(2)}, u32[]{:S(2)}) collective-permute-start(f32[3,2,32,256]{3,2,1,0:T(8,128)S(1)} %get-tuple-element.210), channel_id=1, source_target_pairs={{0,4},{4,8},{8,12},{12,16},{16,20},{20,24},{24,28},{1,5},{5,9},{9,... | collective-permute-start | bytes 589832 | tf_op jit(solution)/shard_map/ppermute | solution.py:27
  76.8 17.2 %collective-permute-start.6 = (f32[3,12,2,256]{3,2,1,0:T(2,128)S(1)}, f32[3,12,2,256]{3,2,1,0:T(2,128)S(1)}, u32[]{:S(2)}, u32[]{:S(2)}) collective-permute-start(f32[3,12,2,256]{3,2,1,0:T(2,128)S(1)} %get-tuple-element.186), channel_id=1, source_target_pairs={{0,1},{1,2},{2,3},{4,5},{5,6},{6,7},{8,9},{9,10},{10,11},{12,13},{... | collective-permute-start | bytes 221192 | tf_op jit(solution)/shard_map/ppermute | solution.py:27
  81.1 12.9 %collective-permute-start.7 = (f32[3,12,2,256]{3,2,1,0:T(2,128)S(1)}, f32[3,12,2,256]{3,2,1,0:T(2,128)S(1)}, u32[]{:S(2)}, u32[]{:S(2)}) collective-permute-start(f32[3,12,2,256]{3,2,1,0:T(2,128)S(1)} %get-tuple-element.187), channel_id=1, source_target_pairs={{1,0},{2,1},{3,2},{5,4},{6,5},{7,6},{9,8},{10,9},{11,10},{13,12},{... | collective-permute-start | bytes 221192 | tf_op jit(solution)/shard_map/ppermute | solution.py:29
  128.5 86.3 %copy-start = (f32[3,8,32,256]{3,2,1,0:T(8,128)}, f32[3,8,32,256]{3,2,1,0:T(8,128)S(1)}, u32[]{:S(2)}) copy-start(f32[3,8,32,256]{3,2,1,0:T(8,128)S(1)} %get-tuple-element.25) | copy-start | bytes 2359300
  128.7 9.6 %copy-start.159 = (pred[16]{0:T(512)(128)(4,1)S(1)}, pred[16]{0:T(512)(128)(4,1)}, u32[]{:S(2)}) copy-start(pred[16]{0:T(512)(128)(4,1)} %get-tuple-element.23) | copy-start | bytes 52
  131.1 125.4 %all-gather.11.cloned.1.call-start = ((), (), s32[]{:S(2)}) async-start(), calls=%async_computation.2 | async-start | bytes 1622016 | tf_op jit(solution)/shard_map/all_gather | solution.py:167
  131.9 7.1 %collective-permute-start.9 = (f32[3,2,32,256]{3,2,1,0:T(8,128)S(1)}, f32[3,2,32,256]{3,2,1,0:T(8,128)S(1)}, u32[]{:S(2)}, u32[]{:S(2)}) collective-permute-start(f32[3,2,32,256]{3,2,1,0:T(8,128)S(1)} %get-tuple-element.204), channel_id=1, source_target_pairs={{4,0},{8,4},{12,8},{16,12},{20,16},{24,20},{28,24},{5,1},{9,5},{13... | collective-permute-start | bytes 589832 | tf_op jit(solution)/shard_map/ppermute | solution.py:29
  133.2 5.8 %collective-permute-start.8 = (f32[3,2,32,256]{3,2,1,0:T(8,128)S(1)}, f32[3,2,32,256]{3,2,1,0:T(8,128)S(1)}, u32[]{:S(2)}, u32[]{:S(2)}) collective-permute-start(f32[3,2,32,256]{3,2,1,0:T(8,128)S(1)} %get-tuple-element.203), channel_id=1, source_target_pairs={{0,4},{4,8},{8,12},{12,16},{16,20},{20,24},{24,28},{1,5},{5,9},{9,... | collective-permute-start | bytes 589832 | tf_op jit(solution)/shard_map/ppermute | solution.py:27
  139.0 13.7 %copy-start.22 = (f32[3,2,32,256]{3,2,1,0:T(8,128)}, f32[3,2,32,256]{3,2,1,0:T(8,128)S(1)}, u32[]{:S(2)}) copy-start(f32[3,2,32,256]{3,2,1,0:T(8,128)S(1)} %collective-permute-done.9) | copy-start | bytes 589828
  139.0 11.7 %copy-start.18 = (f32[3,2,32,256]{3,2,1,0:T(8,128)}, f32[3,2,32,256]{3,2,1,0:T(8,128)S(1)}, u32[]{:S(2)}) copy-start(f32[3,2,32,256]{3,2,1,0:T(8,128)S(1)} %collective-permute-done.8) | copy-start | bytes 589828
  139.1 16.9 %collective-permute-start.10 = (f32[3,12,2,256]{3,2,1,0:T(2,128)S(1)}, f32[3,12,2,256]{3,2,1,0:T(2,128)S(1)}, u32[]{:S(2)}, u32[]{:S(2)}) collective-permute-start(f32[3,12,2,256]{3,2,1,0:T(2,128)S(1)} %get-tuple-element.182), channel_id=1, source_target_pairs={{0,1},{1,2},{2,3},{4,5},{5,6},{6,7},{8,9},{9,10},{10,11},{12,13},{... | collective-permute-start | bytes 221192 | tf_op jit(solution)/shard_map/ppermute | solution.py:27
  143.4 12.6 %collective-permute-start.11 = (f32[3,12,2,256]{3,2,1,0:T(2,128)S(1)}, f32[3,12,2,256]{3,2,1,0:T(2,128)S(1)}, u32[]{:S(2)}, u32[]{:S(2)}) collective-permute-start(f32[3,12,2,256]{3,2,1,0:T(2,128)S(1)} %get-tuple-element.183), channel_id=1, source_target_pairs={{1,0},{2,1},{3,2},{5,4},{6,5},{7,6},{9,8},{10,9},{11,10},{13,12},{... | collective-permute-start | bytes 221192 | tf_op jit(solution)/shard_map/ppermute | solution.py:29
  165.9 27.2 %copy-start.48 = (f32[32,3,128]{2,0,1:T(8,128)S(1)}, f32[32,3,128]{2,0,1:T(8,128)}, u32[]{:S(2)}) copy-start(f32[32,3,128]{2,0,1:T(8,128)} %copy-done.46) | copy-start | bytes 147460
  198.8 3.8 %copy-start.52 = (f32[256]{0:T(256)S(1)}, f32[256]{0:T(256)}, u32[]{:S(2)}) copy-start(f32[256]{0:T(256)} %copy-done.51) | copy-start | bytes 3076
  198.8 3.8 %copy-start.54 = (f32[256]{0:T(256)S(1)}, f32[256]{0:T(256)}, u32[]{:S(2)}) copy-start(f32[256]{0:T(256)} %copy-done.53) | copy-start | bytes 3076
  198.9 3.8 %copy-start.63 = (f32[8,32]{1,0:T(8,128)S(1)}, f32[8,32]{1,0:T(8,128)}, u32[]{:S(2)}) copy-start(f32[8,32]{1,0:T(8,128)} %copy-done.61) | copy-start | bytes 3076
  202.7 3.0 %copy-start.9 = (pred[1,8,32,256]{3,2,1,0:T(8,128)(4,1)S(1)}, pred[1,8,32,256]{3,2,1,0:T(8,128)(4,1)}, u32[]{:S(2)}) copy-start(pred[1,8,32,256]{3,2,1,0:T(8,128)(4,1)} %copy-done.7) | copy-start | bytes 196612
  202.7 3.0 %copy-start.34 = (f32[3,8,32,255]{3,2,1,0:T(8,128)S(1)}, f32[3,8,32,255]{3,2,1,0:T(8,128)}, u32[]{:S(2)}) copy-start(f32[3,8,32,255]{3,2,1,0:T(8,128)} %get-tuple-element.152) | copy-start | bytes 2350084
  202.7 3.0 %copy-start.35 = (f32[3,8,32,255]{3,2,1,0:T(8,128)S(1)}, f32[3,8,32,255]{3,2,1,0:T(8,128)}, u32[]{:S(2)}) copy-start(f32[3,8,32,255]{3,2,1,0:T(8,128)} %get-tuple-element.155) | copy-start | bytes 2350084
  202.7 3.0 %copy-start.50 = (f32[256]{0:T(256)S(1)}, f32[256]{0:T(256)}, u32[]{:S(2)}) copy-start(f32[256]{0:T(256)} %copy-done.49) | copy-start | bytes 3076
  202.7 3.0 %copy-start.85 = (f32[8,32]{1,0:T(8,128)S(1)}, f32[8,32]{1,0:T(8,128)}, u32[]{:S(2)}) copy-start(f32[8,32]{1,0:T(8,128)} %copy-done.82) | copy-start | bytes 3076
  214.8 3.0 %copy-start.114 = (f32[3]{0:T(128)S(1)}, f32[3]{0:T(128)}, u32[]{:S(2)}) copy-start(f32[3]{0:T(128)} %constant.1031.clone) | copy-start | bytes 40
  214.8 3.0 %copy-start.116 = (f32[3]{0:T(128)S(1)}, f32[3]{0:T(128)}, u32[]{:S(2)}) copy-start(f32[3]{0:T(128)} %constant.1029.clone) | copy-start | bytes 40
  214.8 3.0 %copy-start.118 = (f32[3]{0:T(128)S(1)}, f32[3]{0:T(128)}, u32[]{:S(2)}) copy-start(f32[3]{0:T(128)} %constant.1028.clone) | copy-start | bytes 40
  214.8 3.0 %copy-start.120 = (f32[3]{0:T(128)S(1)}, f32[3]{0:T(128)}, u32[]{:S(2)}) copy-start(f32[3]{0:T(128)} %constant.1027.clone) | copy-start | bytes 40
  214.9 3.0 %copy-start.122 = (f32[3]{0:T(128)S(1)}, f32[3]{0:T(128)}, u32[]{:S(2)}) copy-start(f32[3]{0:T(128)} %constant.1026.clone) | copy-start | bytes 40
  214.9 3.0 %copy-start.124 = (f32[3]{0:T(128)S(1)}, f32[3]{0:T(128)}, u32[]{:S(2)}) copy-start(f32[3]{0:T(128)} %constant.1025.clone) | copy-start | bytes 40
  214.9 3.0 %copy-start.126 = (f32[3]{0:T(128)S(1)}, f32[3]{0:T(128)}, u32[]{:S(2)}) copy-start(f32[3]{0:T(128)} %constant.1024.clone) | copy-start | bytes 40
  214.9 3.0 %copy-start.128 = (f32[3]{0:T(128)S(1)}, f32[3]{0:T(128)}, u32[]{:S(2)}) copy-start(f32[3]{0:T(128)} %constant.1023.clone) | copy-start | bytes 40
  214.9 3.0 %copy-start.130 = (f32[3]{0:T(128)S(1)}, f32[3]{0:T(128)}, u32[]{:S(2)}) copy-start(f32[3]{0:T(128)} %constant.1022.clone) | copy-start | bytes 40
  214.9 3.0 %copy-start.132 = (f32[3]{0:T(128)S(1)}, f32[3]{0:T(128)}, u32[]{:S(2)}) copy-start(f32[3]{0:T(128)} %constant.1021.clone) | copy-start | bytes 40
  214.9 2.9 %copy-start.134 = (f32[3]{0:T(128)S(1)}, f32[3]{0:T(128)}, u32[]{:S(2)}) copy-start(f32[3]{0:T(128)} %constant.1020.clone) | copy-start | bytes 40
  224.8 33.2 %copy-start.55 = (f32[32,3,128]{2,0,1:T(8,128)S(1)}, f32[32,3,128]{2,0,1:T(8,128)}, u32[]{:S(2)}) copy-start(f32[32,3,128]{2,0,1:T(8,128)} %reduce_sum.115) | copy-start | bytes 147460
  224.9 33.2 %copy-start.56 = (f32[32,3,128]{2,0,1:T(8,128)S(1)}, f32[32,3,128]{2,0,1:T(8,128)}, u32[]{:S(2)}) copy-start(f32[32,3,128]{2,0,1:T(8,128)} %get-tuple-element.30) | copy-start | bytes 147460
  (123 other events, 206.6 us)
Sparse Core Ops, SparseCore 0:
  22.4 57.8 all-gather.6
  131.2 59.7 all-gather.8
  202.8 53.7 all-gather.10
